TPU v7x, 32 devices: a whole 2x2x4 slice. The times are simulated.
32 devices in a mesh: dp: 8 (over y, x, core), blk: 4 (over z).
Axes of the slice: x: 2, y: 2, z: 4, core: 2. Of those that a mesh axis runs over, the one named last changes fastest.
Arguments:
- tokens: bfloat16 [24, 1024, 1024], P('dp', 'blk'), may hold values from -6 to 6
- cotangent: bfloat16 [24, 1024, 1024], P('dp', 'blk'), may hold values from -6 to 6
- domain_ids: int32 [24, 1024], P('dp', 'blk'), may hold values from 0 to 21
- domain_weight: float32 [22], replicated, may hold values from 0.3 to 3
- frozen_input_weights: bfloat16 [1024, 8192], P('dp'), may hold values from -0.1875 to 0.1875
- bias_in: bfloat16 [8192], replicated, may hold values from -1.25 to 1.25
- frozen_down_weight: bfloat16 [4096, 1024], P('dp'), may hold values from -0.09375 to 0.09375
- bias_ff: bfloat16 [1024], replicated, may hold values from -1.25 to 1.25
- norm_gain: float32 [2, 1024], replicated, may hold values from 0.5 to 1.5
- norm_shift: float32 [2, 1024], replicated, may hold values from -1.25 to 1.25
- adapt_a: float32 [1024, 384], P('dp'), may hold values from -0.1875 to 0.1875
- adapt_a_ff: float32 [4096, 128], P('dp'), may hold values from -0.09375 to 0.09375
- adapt_b: float32 [128, 8192], P(None, 'dp'), may hold values from -0.5 to 0.5
- adapt_b_ff: float32 [128, 1024], P(None, 'dp'), may hold values from -0.5 to 0.5
- mean_a: float32 [1024, 384], P('dp'), may hold values from -192 to 192
- mean_a_ff: float32 [4096, 128], P('dp'), may hold values from -192 to 192
- mean_b: float32 [128, 8192], P(None, 'dp'), may hold values from -192 to 192
- mean_b_ff: float32 [128, 1024], P(None, 'dp'), may hold values from -192 to 192
- square_a: float32 [1024, 384], P('dp'), may hold values from 100 to 100000
- square_a_ff: float32 [4096, 128], P('dp'), may hold values from 100 to 100000
- square_b: float32 [128, 8192], P(None, 'dp'), may hold values from 100 to 100000
- square_b_ff: float32 [128, 1024], P(None, 'dp'), may hold values from 100 to 100000
- keep_a: int32 [1024, 384], P('dp'), may hold values 0 or 1
- keep_a_ff: int32 [4096, 128], P('dp'), may hold values 0 or 1
- keep_b: int32 [128, 8192], P(None, 'dp'), may hold values 0 or 1
- keep_b_ff: int32 [128, 1024], P(None, 'dp'), may hold values 0 or 1
Outputs:
- mixed: bfloat16 [24, 1024, 1024], P('dp', 'blk')
- grad_tokens: bfloat16 [24, 1024, 1024], P('dp', 'blk')
- grad_gain: float32 [2, 1024], replicated
- grad_shift: float32 [2, 1024], replicated
- grad_a: float32 [1024, 384], P('dp')
- grad_a_ff: float32 [4096, 128], P('dp')
- grad_b: float32 [128, 8192], P(None, 'dp')
- grad_b_ff: float32 [128, 1024], P(None, 'dp')
- new_mean_a: float32 [1024, 384], P('dp')
- new_square_a: float32 [1024, 384], P('dp')
- new_mean_a_ff: float32 [4096, 128], P('dp')
- new_square_a_ff: float32 [4096, 128], P('dp')
- new_mean_b: float32 [128, 8192], P(None, 'dp')
- new_square_b: float32 [128, 8192], P(None, 'dp')
- new_mean_b_ff: float32 [128, 1024], P(None, 'dp')
- new_square_b_ff: float32 [128, 1024], P(None, 'dp')
- folded_input_weights: bfloat16 [1024, 8192], P('dp')
- folded_down_weight: bfloat16 [4096, 1024], P('dp')
All inputs are finite; a program needn't handle non-finite values. No bound on the sum of `keep_a` or of `keep_a_ff` or of `keep_b` or of `keep_b_ff` on one device may be relied on, other than what follows from the above.
Results may differ from a plain program's by a relative error of at most 0.025.
Values may be sent and summed in bfloat16 or wider, within the bound.
A program may use at most 320 MiB of HBM per device.

v0:
```python
import math
import jax
import jax.numpy as jnp
from jax import lax
from jax.sharding import PartitionSpec as P

HEADS = 16
ROTARY = 16
DOMAINS = 22
highest = lax.Precision.HIGHEST
adapter_scale = 0.25
rope_base = 10000.0
norm_eps = 1e-05
masked_score = -1e30
first_fix = 1.0 - (0.9**10) ** 10
second_fix = 1.0 - (0.999**10) ** 10


def matrix_product(left, right):
    return jnp.dot(left, right, preferred_element_type=jnp.float32)


def product_right_transposed(left, right):
    return lax.dot_general(
        left, right, (((1,), (1,)), ((), ())), preferred_element_type=jnp.float32
    )


def product_left_transposed(left, right):
    return lax.dot_general(
        left, right, (((0,), (0,)), ((), ())), preferred_element_type=jnp.float32
    )


def precise_product(left, right):
    return jnp.dot(left, right, precision=highest)


def layer_norm(values, gain, shift):
    centre = values - jnp.mean(values, axis=-1, keepdims=True)
    spread = jnp.mean(centre * centre, axis=-1, keepdims=True)
    return centre * lax.rsqrt(spread + norm_eps) * gain + shift


def exact_gelu(values):
    return jax.nn.gelu(values, approximate=False)


def rope_tables(positions, rotary):
    half = rotary // 2
    freqs = rope_base ** (-(jnp.arange(half, dtype=jnp.float32) * 2.0) / rotary)
    angles = positions.astype(jnp.float32)[:, None] * freqs[None, :]
    return (jnp.cos(angles), jnp.sin(angles))


def rotate(values, cosine, sine, rotary):
    half = rotary // 2
    front = values[..., :half]
    back = values[..., half:rotary]
    rest = values[..., rotary:]
    cos_b = cosine[:, None, :]
    sin_b = sine[:, None, :]
    return jnp.concatenate(
        [front * cos_b - back * sin_b, back * cos_b + front * sin_b, rest], axis=-1
    )


def project(input_rows, weight_matrix, bias_vector, down, upper_factor):
    middle_rows = matrix_product(input_rows, down).astype(jnp.bfloat16)
    return (
        matrix_product(input_rows, weight_matrix)
        + bias_vector.astype(jnp.float32)
        + adapter_scale * matrix_product(middle_rows, upper_factor),
        middle_rows,
    )


def project_back(
    output_gradient, input_rows, middle_rows, weight_matrix, bias_vector, down, upper_factor
):
    middle_gradient = (
        adapter_scale * product_right_transposed(output_gradient, upper_factor)
    ).astype(jnp.bfloat16)
    upper_gradient = adapter_scale * product_left_transposed(middle_rows, output_gradient)
    grad_down = product_left_transposed(input_rows, middle_gradient)
    grad_in = product_right_transposed(output_gradient, weight_matrix) + product_right_transposed(
        middle_gradient, down
    )
    return (grad_in, grad_down, upper_gradient)


def split_blocks(full, bias_in, bias_ff, width, rank):
    w_all, w_ff, a_all, a_ff, b_all, b_ff = full
    part_qkv = (w_all[:, : 3 * width], bias_in[: 3 * width], a_all[:, :rank], b_all[:, : 3 * width])
    part_att = (
        w_all[:, 3 * width : 4 * width],
        bias_in[3 * width : 4 * width],
        a_all[:, rank : 2 * rank],
        b_all[:, 3 * width : 4 * width],
    )
    part_up = (
        w_all[:, 4 * width :],
        bias_in[4 * width :],
        a_all[:, 2 * rank :],
        b_all[:, 4 * width :],
    )
    part_ff = (w_ff, bias_ff, a_ff, b_ff)
    return (part_qkv, part_att, part_up, part_ff)


def adam_update(param, grad, mean, square, keep):
    mean_new = 0.9 * mean + 0.1 * grad
    square_new = 0.999 * square + 0.001 * grad * grad
    fresh = param - 0.01 * (mean_new / first_fix) / (jnp.sqrt(square_new / second_fix) + 1e-08)
    kept = keep.astype(jnp.float32)
    return (fresh, mean_new * kept, square_new * kept)


def body(
    tokens,
    cotangent,
    domain_ids,
    domain_weight,
    frozen_input_weights,
    bias_in,
    frozen_down_weight,
    bias_ff,
    norm_gain,
    norm_shift,
    adapt_a,
    adapt_a_ff,
    adapt_b,
    adapt_b_ff,
    mean_a,
    mean_a_ff,
    mean_b,
    mean_b_ff,
    square_a,
    square_a_ff,
    square_b,
    square_b_ff,
    keep_a,
    keep_a_ff,
    keep_b,
    keep_b_ff,
):
    seqs, span, width = tokens.shape
    rows = seqs * span
    rank = adapt_b.shape[0]
    depth = width // HEADS
    att_scale = 1.0 / math.sqrt(depth)
    shards = (
        frozen_input_weights,
        frozen_down_weight,
        adapt_a.astype(jnp.bfloat16),
        adapt_a_ff.astype(jnp.bfloat16),
        adapt_b.astype(jnp.bfloat16),
        adapt_b_ff.astype(jnp.bfloat16),
    )
    whole = (
        lax.all_gather(shards[0], "dp", axis=0, tiled=True),
        lax.all_gather(shards[1], "dp", axis=0, tiled=True),
        lax.all_gather(shards[2], "dp", axis=0, tiled=True),
        lax.all_gather(shards[3], "dp", axis=0, tiled=True),
        lax.all_gather(shards[4], "dp", axis=1, tiled=True),
        lax.all_gather(shards[5], "dp", axis=1, tiled=True),
    )
    part_qkv, part_att, part_up, part_ff = split_blocks(whole, bias_in, bias_ff, width, rank)
    input_rows = tokens.astype(jnp.float32).reshape(rows, width)
    first_f, first_pull = jax.vjp(layer_norm, input_rows, norm_gain[0], norm_shift[0])
    second_f, second_pull = jax.vjp(layer_norm, input_rows, norm_gain[1], norm_shift[1])
    first = first_f.astype(jnp.bfloat16)
    second = second_f.astype(jnp.bfloat16)
    joint, middle_qkv = project(first, *part_qkv)
    joint3 = joint.reshape(seqs, span, 3 * width)
    positions = lax.axis_index("blk") * span + jnp.arange(span, dtype=jnp.int32)
    cosine, sine = rope_tables(positions, ROTARY)

    def turn(query_raw, key_raw):
        return (rotate(query_raw, cosine, sine, ROTARY), rotate(key_raw, cosine, sine, ROTARY))

    (query_r, key_r), rope_pull = jax.vjp(
        turn,
        joint3[..., :width].reshape(seqs, span, HEADS, depth),
        joint3[..., width : 2 * width].reshape(seqs, span, HEADS, depth),
    )
    query_b = query_r.astype(jnp.bfloat16)
    key_local = key_r.astype(jnp.bfloat16)
    value_local = joint3[..., 2 * width :].reshape(seqs, span, HEADS, depth).astype(jnp.bfloat16)
    key_send = key_local.reshape(seqs, span, width)
    value_send = value_local.reshape(seqs, span, width)
    top = jnp.full((seqs, HEADS, span), masked_score, jnp.float32)
    key_piece = lax.all_gather(key_send, "blk", axis=1, tiled=True)
    value_piece = lax.all_gather(value_send, "blk", axis=1, tiled=True)
    count = key_piece.shape[1]
    key_h = key_piece.reshape(seqs, count, HEADS, depth)
    value_h = value_piece.reshape(seqs, count, HEADS, depth)
    scores = (
        jnp.einsum("sqhe,skhe->shqk", query_b, key_h, preferred_element_type=jnp.float32)
        * att_scale
    )
    allowed = positions[:, None] >= jnp.arange(count, dtype=jnp.int32)[None, :]
    scores = jnp.where(allowed, scores, masked_score)
    new_top = jnp.maximum(top, jnp.max(scores, axis=-1))
    weights = jnp.where(allowed, jnp.exp(scores - new_top[..., None]), 0.0)
    total = jnp.sum(weights, axis=-1)
    update = jnp.einsum(
        "shqk,skhe->sqhe", weights.astype(jnp.bfloat16), value_h, preferred_element_type=jnp.float32
    )
    accum = update
    top, total, accum = (new_top, total, accum)
    attended_f = (accum / jnp.transpose(total, (0, 2, 1))[..., None]).reshape(rows, width)
    log_total = top + jnp.log(total)
    attended = attended_f.astype(jnp.bfloat16)
    branch_att, middle_att = project(attended, *part_att)
    up_pre, middle_up = project(second, *part_up)
    hidden_f, gelu_pull = jax.vjp(exact_gelu, up_pre)
    hidden = hidden_f.astype(jnp.bfloat16)
    branch_ff, middle_ff = project(hidden, *part_ff)
    mixed = (input_rows + branch_att + branch_ff).astype(jnp.bfloat16).reshape(seqs, span, width)
    lookup = (domain_ids[..., None] == jnp.arange(DOMAINS, dtype=jnp.int32)).astype(jnp.float32)
    row_weight = jnp.sum(lookup * domain_weight, axis=-1).reshape(rows, 1)
    row_grad = cotangent.astype(jnp.float32).reshape(rows, width) * row_weight
    grad_low = row_grad.astype(jnp.bfloat16)
    grad_hidden, grad_a_ffp, grad_b_ffp = project_back(grad_low, hidden, middle_ff, *part_ff)
    upper_gradient = gelu_pull(grad_hidden)[0].astype(jnp.bfloat16)
    grad_second, grad_a_up, grad_b_up = project_back(upper_gradient, second, middle_up, *part_up)
    grad_att_f, grad_a_att, grad_b_att = project_back(grad_low, attended, middle_att, *part_att)
    grad_att = grad_att_f.astype(jnp.bfloat16)
    grad_heads = grad_att.reshape(seqs, span, HEADS, depth)
    delta = jnp.transpose(
        jnp.sum(
            grad_heads.astype(jnp.float32) * attended_f.reshape(seqs, span, HEADS, depth), axis=-1
        ),
        (0, 2, 1),
    )
    key_piece = lax.all_gather(key_send, "blk", axis=1, tiled=True)
    value_piece = lax.all_gather(value_send, "blk", axis=1, tiled=True)
    count = key_piece.shape[1]
    key_h = key_piece.reshape(seqs, count, HEADS, depth)
    value_h = value_piece.reshape(seqs, count, HEADS, depth)
    scores = (
        jnp.einsum("sqhe,skhe->shqk", query_b, key_h, preferred_element_type=jnp.float32)
        * att_scale
    )
    allowed = positions[:, None] >= jnp.arange(count, dtype=jnp.int32)[None, :]
    weights = jnp.where(allowed, jnp.exp(scores - log_total[..., None]), 0.0)
    grad_w = jnp.einsum("sqhe,skhe->shqk", grad_heads, value_h, preferred_element_type=jnp.float32)
    grad_s = (weights * (grad_w - delta[..., None])).astype(jnp.bfloat16)
    grad_query = (
        jnp.einsum("shqk,skhe->sqhe", grad_s, key_h, preferred_element_type=jnp.float32) * att_scale
    )
    stats_lse, stats_delta = (
        lax.all_gather(log_total.astype(jnp.bfloat16), "blk", axis=2, tiled=True).astype(
            log_total.dtype
        ),
        lax.all_gather(delta.astype(jnp.bfloat16), "blk", axis=2, tiled=True).astype(delta.dtype),
    )
    query_piece = lax.all_gather(query_b.reshape(seqs, span, width), "blk", axis=1, tiled=True)
    grad_piece = lax.all_gather(grad_att.reshape(seqs, span, width), "blk", axis=1, tiled=True)
    count = query_piece.shape[1]
    query_h = query_piece.reshape(seqs, count, HEADS, depth)
    grad_h = grad_piece.reshape(seqs, count, HEADS, depth)
    scores = (
        jnp.einsum("sqhe,skhe->shqk", query_h, key_local, preferred_element_type=jnp.float32)
        * att_scale
    )
    allowed = jnp.arange(count, dtype=jnp.int32)[:, None] >= positions[None, :]
    weights = jnp.where(allowed, jnp.exp(scores - stats_lse[..., None]), 0.0)
    grad_v = jnp.einsum(
        "shqk,sqhe->skhe", weights.astype(jnp.bfloat16), grad_h, preferred_element_type=jnp.float32
    )
    grad_w = jnp.einsum("sqhe,skhe->shqk", grad_h, value_local, preferred_element_type=jnp.float32)
    grad_s = (weights * (grad_w - stats_delta[..., None])).astype(jnp.bfloat16)
    grad_k = (
        jnp.einsum("shqk,sqhe->skhe", grad_s, query_h, preferred_element_type=jnp.float32)
        * att_scale
    )
    grad_query_raw, grad_key_raw = rope_pull((grad_query, grad_k))
    grad_joint = jnp.concatenate(
        [
            grad_query_raw.reshape(rows, width),
            grad_key_raw.reshape(rows, width),
            grad_v.reshape(rows, width),
        ],
        axis=1,
    ).astype(jnp.bfloat16)
    grad_first, grad_a_qkv, grad_b_qkv = project_back(grad_joint, first, middle_qkv, *part_qkv)
    back_one = first_pull(grad_first)
    back_two = second_pull(grad_second)
    grad_tokens = (
        (row_grad + back_one[0] + back_two[0]).astype(jnp.bfloat16).reshape(seqs, span, width)
    )
    gain_part = jnp.stack([back_one[1], back_two[1]])
    shift_part = jnp.stack([back_one[2], back_two[2]])
    grad_a_part = jnp.concatenate([grad_a_qkv, grad_a_att, grad_a_up], axis=1)
    grad_b_part = jnp.concatenate([grad_b_qkv, grad_b_att, grad_b_up], axis=1)
    summed = lax.psum(
        (grad_a_part, grad_a_ffp, grad_b_part, grad_b_ffp, gain_part, shift_part), ("dp", "blk")
    )
    owner = lax.axis_index("dp")
    grad_a = lax.dynamic_slice_in_dim(summed[0], owner * adapt_a.shape[0], adapt_a.shape[0], 0)
    grad_a_ff = lax.dynamic_slice_in_dim(
        summed[1], owner * adapt_a_ff.shape[0], adapt_a_ff.shape[0], 0
    )
    grad_b = lax.dynamic_slice_in_dim(summed[2], owner * adapt_b.shape[1], adapt_b.shape[1], 1)
    grad_b_ff = lax.dynamic_slice_in_dim(
        summed[3], owner * adapt_b_ff.shape[1], adapt_b_ff.shape[1], 1
    )
    grad_gain = summed[4]
    grad_shift = summed[5]
    fresh_a, new_mean_a, new_square_a = adam_update(adapt_a, grad_a, mean_a, square_a, keep_a)
    reset_down_adapter_left, new_mean_a_ff, new_square_a_ff = adam_update(
        adapt_a_ff, grad_a_ff, mean_a_ff, square_a_ff, keep_a_ff
    )
    fresh_b, new_mean_b, new_square_b = adam_update(adapt_b, grad_b, mean_b, square_b, keep_b)
    reset_down_adapter_right, new_mean_b_ff, new_square_b_ff = adam_update(
        adapt_b_ff, grad_b_ff, mean_b_ff, square_b_ff, keep_b_ff
    )
    fresh_b_all, reset_down_right_stacked = (
        lax.all_gather(fresh_b.astype(jnp.bfloat16), "dp", axis=1, tiled=True).astype(
            fresh_b.dtype
        ),
        lax.all_gather(
            reset_down_adapter_right.astype(jnp.bfloat16), "dp", axis=1, tiled=True
        ).astype(reset_down_adapter_right.dtype),
    )
    input_weight_update = jnp.concatenate(
        [
            precise_product(fresh_a[:, :rank], fresh_b_all[:, : 3 * width]),
            precise_product(fresh_a[:, rank : 2 * rank], fresh_b_all[:, 3 * width : 4 * width]),
            precise_product(fresh_a[:, 2 * rank :], fresh_b_all[:, 4 * width :]),
        ],
        axis=1,
    )
    folded_input_weights = (
        frozen_input_weights.astype(jnp.float32) + adapter_scale * input_weight_update
    ).astype(jnp.bfloat16)
    folded_down_weight = (
        frozen_down_weight.astype(jnp.float32)
        + adapter_scale * precise_product(reset_down_adapter_left, reset_down_right_stacked)
    ).astype(jnp.bfloat16)
    return (
        mixed,
        grad_tokens,
        grad_gain,
        grad_shift,
        grad_a,
        grad_a_ff,
        grad_b,
        grad_b_ff,
        new_mean_a,
        new_square_a,
        new_mean_a_ff,
        new_square_a_ff,
        new_mean_b,
        new_square_b,
        new_mean_b_ff,
        new_square_b_ff,
        folded_input_weights,
        folded_down_weight,
    )


def solution(mesh):
    in_specs = (
        P("dp", "blk", None),
        P("dp", "blk", None),
        P("dp", "blk"),
        P(),
        P("dp", None),
        P(),
        P("dp", None),
        P(),
        P(),
        P(),
        P("dp", None),
        P("dp", None),
        P(None, "dp"),
        P(None, "dp"),
        P("dp", None),
        P("dp", None),
        P(None, "dp"),
        P(None, "dp"),
        P("dp", None),
        P("dp", None),
        P(None, "dp"),
        P(None, "dp"),
        P("dp", None),
        P("dp", None),
        P(None, "dp"),
        P(None, "dp"),
    )
    out_specs = (
        P("dp", "blk", None),
        P("dp", "blk", None),
        P(),
        P(),
        P("dp", None),
        P("dp", None),
        P(None, "dp"),
        P(None, "dp"),
        P("dp", None),
        P("dp", None),
        P("dp", None),
        P("dp", None),
        P(None, "dp"),
        P(None, "dp"),
        P(None, "dp"),
        P(None, "dp"),
        P("dp", None),
        P("dp", None),
    )
    return jax.shard_map(body, mesh=mesh, in_specs=in_specs, out_specs=out_specs, check_vma=False)
```

profile of v0, /device:TPU:0, one launch (start us, length us, event | category | flops | bytes accessed | tf_op | source)
XLA Modules:
  0.0 990.2 jit_solution(3469510999970349865)
XLA Ops:
  12.5 12.9 %all_gather.45 = bf16[1024,384]{1,0:T(8,128)(2,1)} all-gather(bf16[128,384]{1,0:T(8,128)(2,1)S(1)} %convert_element_type.174), channel_id=1, replica_groups=mesh['dp'=8,'blk'=4] {'dp'}, dimensions={0}, use_global_device_ids=true | all-gather | bytes 884736 | tf_op jit(solution)/shard_map/all_gather | solution.py:163
  30.0 72.5 %all-gather.10.cloned.1.call-done = bf16[1024,8192]{1,0:T(8,128)(2,1)} async-done(((bf16[128,8192]{1,0:T(8,128)(2,1)}), bf16[1024,8192]{1,0:T(8,128)(2,1)}) %all-gather.10.cloned.1.call-update) | async-done | bytes 16777232 | tf_op jit(solution)/shard_map/all_gather | solution.py:161
  112.8 20.2 %all-gather.12.cloned.1.call-done = bf16[128,8192]{1,0:T(8,128)(2,1)} async-done(((bf16[128,1024]{1,0:T(8,128)(2,1)}), bf16[128,8192]{1,0:T(8,128)(2,1)}) %all-gather.12.cloned.1.call-update) | async-done | bytes 2097168 | tf_op jit(solution)/shard_map/all_gather | solution.py:165
  168.0 10.3 %all_gather.51 = bf16[128,1024]{1,0:T(8,128)(2,1)S(1)} all-gather(bf16[128,128]{1,0:T(8,128)(2,1)} %convert_element_type.194), channel_id=1, replica_groups=mesh['dp'=8,'blk'=4] {'dp'}, dimensions={1}, use_global_device_ids=true | all-gather | bytes 294912 | tf_op jit(solution)/shard_map/all_gather | solution.py:166
  190.3 12.6 %fusion.136 = f32[768,4096]{1,0:T(8,128)} fusion(bf16[768,1024]{1,0:T(8,128)(2,1)S(1)} %fusion.28, bf16[4096,1024]{1,0:T(8,128)(2,1)} %all-gather.18.cloned.1.call-done), kind=kOutput, calls=%fused_computation.232 | convolution fusion | flops 6442450944 | bytes 22544384 | tf_op jit(solution)/shard_map/dot_general | solution.py:24
  231.5 31.8 %multiply_convert_fusion.2 = (bf16[768,4096]{1,0:T(8,128)(2,1)}, f32[768,4096]{1,0:T(8,128)}, f32[768,4096]{1,0:T(8,128)}) fusion(bf16[768,128]{1,0:T(8,128)(2,1)S(1)} %copy-done.54, bf16[128,8192]{1,0:T(8,128)(2,1)S(1)} %copy-done.56, f32[768,4096]{1,0:T(8,128)S(1)} %fusion.19, f32[4096]{0:T(1024)S(1)} %copy-done.84), kind=kOutput, calls=%fused_computation.15 | convolution fusion | flops 1019215872 | bytes 45301760 | tf_op jit(solution)/shard_map/dot_general | solution.py:20
  263.4 17.3 %add_convert_fusion = bf16[768,4096]{1,0:T(8,128)(2,1)} fusion(f32[768,4096]{1,0:T(8,128)} %get-tuple-element.99, f32[768,4096]{1,0:T(8,128)} %fusion.136, f32[768,4096]{1,0:T(8,128)} %get-tuple-element.136, bf16[768,128]{1,0:T(8,128)(2,1)} %fusion.69, bf16[4096,128]{1,0:T(8,128)(2,1)} %all-gather.20.cloned.1.call-done), kind=kOutput, calls=%fused_computation.14 | convolution fusion | flops 852492288 | bytes 45285376 | tf_op jit(solution)/shard_map/dot_general | solution.py:24
  298.8 12.6 %fusion.135 = f32[768,1024]{1,0:T(8,128)} fusion(bf16[768,4096]{1,0:T(8,128)(2,1)} %get-tuple-element.98, bf16[4096,1024]{1,0:T(8,128)(2,1)} %all-gather.18.cloned.1.call-done), kind=kOutput, calls=%fused_computation.231 | convolution fusion | flops 6442450944 | bytes 17825792 | tf_op jit(solution)/shard_map/dot_general | solution.py:20
  311.4 21.1 %all-gather.16.cloned.1.call-done = bf16[3,1024,1024]{1,2,0:T(8,128)(2,1)} async-done(((bf16[3,256,1024]{1,2,0:T(8,128)(2,1)}), bf16[3,1024,1024]{1,2,0:T(8,128)(2,1)}) %all-gather.16.cloned.1.call-update) | async-done | bytes 6291472 | tf_op jit(solution)/shard_map/all_gather | solution.py:193
  332.5 21.8 %select_reduce_fusion = (f32[3,16,256]{2,1,0:T(8,128)S(1)}, f32[3,16,256,1024]{3,2,1,0:T(8,128)}) fusion(pred[256,1024]{1,0:T(8,128)(4,1)S(1)} %copy-done.5, bf16[3,1024,16,64]{1,3,2,0:T(8,128)(2,1)} %bitcast.174, bf16[3,256,16,48]{1,3,2,0:T(8,128)(2,1)S(1)} %copy-done.14, bf16[3,256,16,8]{1,3,2,0:T(8,128)(2,1)S(1)} %get-tuple-element.124, ...), kind=kOutput, calls=%fused_computation.4 | convolution fusion | flops 1653067776 | bytes 58507264 | tf_op jit(solution)/shard_map/sqhe,skhe->shqk/dot_general | solution.py:199
  354.3 23.0 %fusion.1 = f32[3,16,256]{2,1,0:T(8,128)S(1)} fusion(f32[3,16,256,1024]{3,2,1,0:T(8,128)} %get-tuple-element.135, f32[3,16,256]{2,1,0:T(8,128)S(1)} %broadcast_maximum_fusion, pred[256,1024]{1,0:T(8,128)(4,1)S(1)} %copy-done.5), kind=kLoop, calls=%fused_computation.6 | loop fusion | flops 62902272 | bytes 50692096 | tf_op jit(solution)/shard_map/reduce_sum | solution.py:206
  377.3 20.7 %all_gather.53 = bf16[3,16,1024]{2,1,0:T(8,128)(2,1)S(1)} all-gather(bf16[3,16,256]{2,1,0:T(8,128)(2,1)S(1)} %get-tuple-element.96), channel_id=1, replica_groups=mesh['dp'=8,'blk'=4] {'blk'}, dimensions={2}, use_global_device_ids=true | all-gather | bytes 122880 | tf_op jit(solution)/shard_map/all_gather | solution.py:254
  398.0 50.5 %all-gather.14.cloned.1.call-done = bf16[3,1024,1024]{1,2,0:T(8,128)(2,1)} async-done(((bf16[3,256,1024]{1,2,0:T(8,128)(2,1)}), bf16[3,1024,1024]{1,2,0:T(8,128)(2,1)}) %all-gather.14.cloned.1.call-update) | async-done | bytes 6291472 | tf_op jit(solution)/shard_map/all_gather | solution.py:194
  448.5 23.5 %multiply_reduce_fusion = (f32[3,256,16]{1,2,0:T(8,128)S(1)}, bf16[3,256,16,64]{1,3,2,0:T(8,128)(2,1)}) fusion(bf16[3,256,16,64]{1,3,2,0:T(8,128)(2,1)S(1)} %copy-done.39, f32[3,256,16]{1,2,0:T(8,128)S(1)} %bitcast.202, bf16[3,1024,16,64]{1,3,2,0:T(8,128)(2,1)} %bitcast.218, f32[3,16,256,1024]{3,2,1,0:T(8,128)} %get-tuple-element.135, ...), kind=kOutput, calls=%fused_computation.86 | convolution fusion | flops 1677447168 | bytes 60178432 | tf_op jit(solution)/shard_map/shqk,skhe->sqhe/dot_general | solution.py:207
  472.1 28.8 %multiply_bitcast_fusion.1 = f32[3,256,16,64]{1,3,2,0:T(8,128)} fusion(bf16[3,1024,16,64]{1,3,2,0:T(8,128)(2,1)} %bitcast.175, f32[3,16,256,1024]{3,2,1,0:T(8,128)} %get-tuple-element.135, bf16[3,256,16,64]{1,3,2,0:T(8,128)(2,1)S(1)} %copy-done.39, bf16[3,1024,16,64]{1,3,2,0:T(8,128)(2,1)} %bitcast.219, f32[3,16,256]{2,1,0:T(8,128)S(1)} %bitcast.211, ...), kind=kOutput, calls=%fused_computation.85 | convolution fusion | flops 3297509376 | bytes 67993600 | tf_op jit(solution)/shard_map/shqk,skhe->sqhe/dot_general | solution.py:251
  500.9 27.6 %all_gather.55 = bf16[3,16,1024]{2,1,0:T(8,128)(2,1)S(1)} all-gather(bf16[3,16,256]{2,1,0:T(8,128)(2,1)S(1)} %bitcast_convert_fusion), channel_id=1, replica_groups=mesh['dp'=8,'blk'=4] {'blk'}, dimensions={2}, use_global_device_ids=true | all-gather | bytes 122880 | tf_op jit(solution)/shard_map/all_gather | solution.py:257
  529.2 35.5 %all-gather.22.cloned.1.call-done = bf16[3,1024,1024]{1,2,0:T(8,128)(2,1)} async-done(((bf16[3,256,1024]{1,2,0:T(8,128)(2,1)}), bf16[3,1024,1024]{1,2,0:T(8,128)(2,1)}) %all-gather.22.cloned.1.call-update) | async-done | bytes 6291472 | tf_op jit(solution)/shard_map/all_gather | solution.py:259
  564.7 22.0 %fusion.134 = f32[3,16,1024,256]{3,2,1,0:T(8,128)} fusion(bf16[3,1024,16,64]{1,3,2,0:T(8,128)(2,1)} %bitcast.179, bf16[3,256,16,48]{1,3,2,0:T(8,128)(2,1)S(1)} %copy-done.13, bf16[3,256,16,8]{1,3,2,0:T(8,128)(2,1)S(1)} %copy-done.36, bf16[3,256,16,8]{1,3,2,0:T(8,128)(2,1)S(1)} %copy-done.34), kind=kOutput, calls=%fused_computation.230 | convolution fusion | flops 1615331328 | bytes 58195968 | tf_op jit(solution)/shard_map/sqhe,skhe->shqk/dot_general | solution.py:265
  586.7 93.3 %all-gather.24.cloned.1.call-done = bf16[3,1024,1024]{2,1,0:T(8,128)(2,1)} async-done(((bf16[3,256,1024]{2,1,0:T(8,128)(2,1)}), bf16[3,1024,1024]{2,1,0:T(8,128)(2,1)}) %all-gather.24.cloned.1.call-update) | async-done | bytes 6291472 | tf_op jit(solution)/shard_map/all_gather | solution.py:260
  688.7 20.5 %fusion.64 = bf16[3,256,16,64]{1,3,2,0:T(8,128)(2,1)} fusion(bf16[3,1024,16,64]{1,3,2,0:T(8,128)(2,1)} %bitcast.189, f32[3,16,1024,256]{3,2,1,0:T(8,128)} %fusion.134, f32[3,16,1024]{2,1,0:T(8,128)S(1)} %convert_element_type.203, pred[1024,256]{1,0:T(8,128)(4,1)S(1)} %copy-done.60), kind=kOutput, calls=%fused_computation.97 | convolution fusion | flops 1661730816 | bytes 58654720 | tf_op jit(solution)/shard_map/shqk,sqhe->skhe/dot_general | solution.py:270
  709.2 28.0 %multiply_bitcast_fusion = f32[3,256,16,64]{1,3,2,0:T(8,128)} fusion(bf16[3,1024,16,64]{1,3,2,0:T(8,128)(2,1)} %bitcast.180, f32[3,16,1024,256]{3,2,1,0:T(8,128)} %fusion.134, bf16[3,1024,16,64]{1,3,2,0:T(8,128)(2,1)} %bitcast.190, bf16[3,256,16,64]{1,3,2,0:T(8,128)(2,1)} %bitcast.191, f32[3,16,1024]{2,1,0:T(8,128)} %convert_element_type.206, ...), kind=kOutput, calls=%fused_computation.83 | convolution fusion | flops 3297509376 | bytes 68288512 | tf_op jit(solution)/shard_map/shqk,sqhe->skhe/dot_general | solution.py:276
  772.9 13.2 %fusion.128 = (f32[1024]{0:T(1024)S(1)}, f32[768]{0:T(1024)S(1)}, f32[768]{0:T(1024)S(1)}, f32[1024]{0:T(1024)S(1)}, f32[768,1024]{1,0:T(8,128)S(1)}) fusion(f32[1024]{0:T(1024)S(1)} %bitcast.208, f32[768]{0:T(1024)S(1)} %copy-done.71, bf16[3,256,1024]{2,1,0:T(8,128)(2,1)S(1)} %copy-done.1, f32[768,1024]{1,0:T(8,128)S(1)} %convolution_add_fusion, ...), kind=kOutput, calls=%fused_computation.225 | convolution fusion | flops 6451097600 | bytes 25715712 | tf_op jit(solution)/shard_map/dot_general | solution.py:24
  789.1 39.3 %all-reduce.6 = (f32[2,1024]{1,0:T(2,128)}, f32[2,1024]{1,0:T(2,128)}) all-reduce(f32[2,1024]{1,0:T(2,128)S(1)} %pad_maximum_fusion.2, f32[2,1024]{1,0:T(2,128)S(1)} %pad_maximum_fusion.3), channel_id=1, replica_groups=mesh['dp'=8,'blk'=4] {'dp','blk'}, use_global_device_ids=true, to_apply=%region_12.13 | all-reduce | flops 4096 | bytes 32768 | tf_op jit(solution)/shard_map/psum | solution.py:298
  836.6 103.6 %all-reduce.10.cloned.1.call-done = (f32[1024,384]{0,1:T(8,128)}, f32[4096,128]{1,0:T(8,128)}, f32[128,8192]{1,0:T(8,128)}, f32[128,1024]{1,0:T(8,128)}) async-done(((f32[1024,384]{0,1:T(8,128)}, f32[4096,128]{1,0:T(8,128)}, f32[128,8192]{1,0:T(8,128)}, f32[128,1024]{1,0:T(8,128)}), (f32[1024,384]{0,1:T(8,128)}, f32[4096,128]{1,0:T(8,128)}, f32[128,8192]{1,0:T(8,128)}, ...) | async-done | bytes 8388624 | tf_op jit(solution)/shard_map/psum | solution.py:298
  (329 shorter events, 211.8 us)
Async XLA Ops:
  7.2 95.3 %all-gather.10.cloned.1.call-start = ((), (), s32[]{:S(2)}) async-start(), calls=%async_computation | async-start | bytes 18874368 | tf_op jit(solution)/shard_map/all_gather | solution.py:161
  8.0 125.0 %all-gather.12.cloned.1.call-start = ((), (), s32[]{:S(2)}) async-start(), calls=%async_computation.1 | async-start | bytes 2359296 | tf_op jit(solution)/shard_map/all_gather | solution.py:165
  9.9 180.5 %all-gather.18.cloned.1.call-start = ((), (), s32[]{:S(2)}) async-start(), calls=%async_computation.4 | async-start | bytes 9437184 | tf_op jit(solution)/shard_map/all_gather | solution.py:162
  10.6 252.8 %all-gather.20.cloned.1.call-start = ((), (), s32[]{:S(2)}) async-start(), calls=%async_computation.5 | async-start | bytes 1179648 | tf_op jit(solution)/shard_map/all_gather | solution.py:164
  11.4 321.1 %all-gather.16.cloned.1.call-start = ((), (), s32[]{:S(2)}) async-start(), calls=%async_computation.3 | async-start | bytes 7864320 | tf_op jit(solution)/shard_map/all_gather | solution.py:193
  28.1 84.6 %copy-start.21 = (bf16[768,1024]{1,0:T(8,128)(2,1)}, bf16[768,1024]{1,0:T(8,128)(2,1)S(1)}, u32[]{:S(2)}) copy-start(bf16[768,1024]{1,0:T(8,128)(2,1)S(1)} %get-tuple-element.112) | copy-start | bytes 4718596
  29.9 103.1 %copy-start.45 = (bf16[768,128]{1,0:T(8,128)(2,1)}, bf16[768,128]{1,0:T(8,128)(2,1)S(1)}, u32[]{:S(2)}) copy-start(bf16[768,128]{1,0:T(8,128)(2,1)S(1)} %convolution_convert_fusion.3) | copy-start | bytes 589828
  30.0 121.2 %copy-start.66 = (f32[256,8]{0,1:T(8,128)}, f32[256,8]{0,1:T(8,128)S(1)}, u32[]{:S(2)}) copy-start(f32[256,8]{0,1:T(8,128)S(1)} %get-tuple-element.132) | copy-start | bytes 24580
  30.0 121.2 %copy-start.68 = (f32[256,8]{0,1:T(8,128)}, f32[256,8]{0,1:T(8,128)S(1)}, u32[]{:S(2)}) copy-start(f32[256,8]{0,1:T(8,128)S(1)} %get-tuple-element.133) | copy-start | bytes 24580
  154.7 293.8 %all-gather.14.cloned.1.call-start = ((), (), s32[]{:S(2)}) async-start(), calls=%async_computation.2 | async-start | bytes 7864320 | tf_op jit(solution)/shard_map/all_gather | solution.py:194
  158.6 406.2 %all-gather.22.cloned.1.call-start = ((), (), s32[]{:S(2)}) async-start(), calls=%async_computation.6 | async-start | bytes 7864320 | tf_op jit(solution)/shard_map/all_gather | solution.py:259
  185.2 103.5 %copy-start.6 = (bf16[768,1024]{1,0:T(8,128)(2,1)}, bf16[768,1024]{1,0:T(8,128)(2,1)S(1)}, u32[]{:S(2)}) copy-start(bf16[768,1024]{1,0:T(8,128)(2,1)S(1)} %fusion.28) | copy-start | bytes 4718596
  221.8 458.3 %all-gather.24.cloned.1.call-start = ((), (), s32[]{:S(2)}) async-start(), calls=%async_computation.7 | async-start | bytes 7864320 | tf_op jit(solution)/shard_map/all_gather | solution.py:260
  298.7 641.4 %all-reduce.10.cloned.1.call-start = ((), (), s32[]{:S(2)}) async-start(), calls=%async_computation.9 | async-start | bytes 16777216 | tf_op jit(solution)/shard_map/psum | solution.py:298
  354.3 94.2 %copy-start.39 = (bf16[3,256,16,64]{1,3,2,0:T(8,128)(2,1)S(1)}, bf16[3,256,16,64]{1,3,2,0:T(8,128)(2,1)}, u32[]{:S(2)}) copy-start(bf16[3,256,16,64]{1,3,2,0:T(8,128)(2,1)} %copy.77) | copy-start | bytes 4718596
  398.0 290.7 %copy-start.64 = (f32[3,16,1024]{2,1,0:T(8,128)}, f32[3,16,1024]{2,1,0:T(8,128)S(1)}, u32[]{:S(2)}) copy-start(f32[3,16,1024]{2,1,0:T(8,128)S(1)} %convert_element_type.203) | copy-start | bytes 589828
  500.9 63.8 %copy-start.34 = (bf16[3,256,16,8]{1,3,2,0:T(8,128)(2,1)S(1)}, bf16[3,256,16,8]{1,3,2,0:T(8,128)(2,1)}, u32[]{:S(2)}) copy-start(bf16[3,256,16,8]{1,3,2,0:T(8,128)(2,1)} %copy-done.33) | copy-start | bytes 589828
  500.9 63.8 %copy-start.36 = (bf16[3,256,16,8]{1,3,2,0:T(8,128)(2,1)S(1)}, bf16[3,256,16,8]{1,3,2,0:T(8,128)(2,1)}, u32[]{:S(2)}) copy-start(bf16[3,256,16,8]{1,3,2,0:T(8,128)(2,1)} %copy-done.35) | copy-start | bytes 589828
  586.7 102.0 %copy-start.60 = (pred[1024,256]{1,0:T(8,128)(4,1)S(1)}, pred[1024,256]{1,0:T(8,128)(4,1)}, u32[]{:S(2)}) copy-start(pred[1024,256]{1,0:T(8,128)(4,1)} %iota_compare_fusion) | copy-start | bytes 786436
  761.6 215.2 %all-gather.26.cloned.1.call-start = ((), (), s32[]{:S(2)}) async-start(), calls=%async_computation.8 | async-start | bytes 2359296 | tf_op jit(solution)/shard_map/all_gather | solution.py:321
  836.6 106.2 %copy-start.41 = (bf16[128,1024]{1,0:T(8,128)(2,1)S(1)}, bf16[128,1024]{1,0:T(8,128)(2,1)}, u32[]{:S(2)}) copy-start(bf16[128,1024]{1,0:T(8,128)(2,1)} %copy-done.40) | copy-start | bytes 786436
  836.6 106.2 %copy-start.53 = (bf16[768,128]{1,0:T(8,128)(2,1)S(1)}, bf16[768,128]{1,0:T(8,128)(2,1)}, u32[]{:S(2)}) copy-start(bf16[768,128]{1,0:T(8,128)(2,1)} %copy-done.52) | copy-start | bytes 589828
  836.6 106.2 %copy-start.82 = (f32[1024]{0:T(1024)S(1)}, f32[1024]{0:T(1024)}, u32[]{:S(2)}) copy-start(f32[1024]{0:T(1024)} %convert_element_type.191) | copy-start | bytes 12292
  836.6 106.2 %copy-start.83 = (f32[1024]{0:T(1024)S(1)}, f32[1024]{0:T(1024)}, u32[]{:S(2)}) copy-start(f32[1024]{0:T(1024)} %slice_convert_fusion.2) | copy-start | bytes 12292
  (81 other events, 823.4 us)
Sparse Core Ops, SparseCore 0:
  9.9 92.5 all-gather.9
  105.0 27.8 all-gather.11
  134.8 55.4 all-gather.17
  192.6 23.4 all-gather.19
  217.6 114.8 all-gather.15
  333.9 114.6 all-gather.13
  450.1 114.6 all-gather.21
  566.3 113.7 all-gather.23
  761.7 178.4 all-reduce.9
  942.9 28.6 all-gather.25
where the time goes:
time: 999 us; the launch traced here: 990 us
  waiting for transfers between devices  400 us (40%)
  matrix products  326 us (33%)
  blocking collectives  121 us (12%)
  other arithmetic  68.4 us (7%)
  local copies, waits for them, and re-layouts  58.5 us (6%)
  between operations  15.7 us (2%)
    psum x1, waiting for transfers between devices, body(): lax.psum((grad_a_part, grad_a_ffp, grad_b_part, grad_b_ffp, gain_part, sh...  104 us
    all_gather x1, waiting for transfers between devices, body(): lax.all_gather(grad_att.reshape(seqs, span, width), 'blk', axis=1, tiled=...  93.3 us
    dot_general x12, matrix products, matrix_product(): return jnp.dot(left, right, preferred_element_type=jnp.float32)  91.1 us
    dot_general x12, matrix products, product_right_transposed(): lax.dot_general(left, right, (((1,), (1,)), ((), ())), preferred_element_...  72.7 us
    all_gather x1, waiting for transfers between devices, body(): lax.all_gather(shards[0], 'dp', axis=0, tiled=True)  72.5 us
    all_gather x1, waiting for transfers between devices, body(): value_piece = lax.all_gather(value_send, 'blk', axis=1, tiled=True)  50.5 us
    psum x1, blocking collectives, body(): lax.psum((grad_a_part, grad_a_ffp, grad_b_part, grad_b_ffp, gain_part, sh...  39.3 us
    all_gather x1, waiting for transfers between devices, body(): lax.all_gather(query_b.reshape(seqs, span, width), 'blk', axis=1, tiled=T...  35.5 us
  transfers between devices with their start and end apart: 10, of which 8 were waited for; matrix products, arithmetic and copies ran while one was open for 36% of the time, Pallas kernels for 0%

commit v1 on v0

--- a/solution.py
+++ b/solution.py
@@ -190,8 +190,11 @@
     key_send = key_local.reshape(seqs, span, width)
     value_send = value_local.reshape(seqs, span, width)
     top = jnp.full((seqs, HEADS, span), masked_score, jnp.float32)
-    key_piece = lax.all_gather(key_send, "blk", axis=1, tiled=True)
-    value_piece = lax.all_gather(value_send, "blk", axis=1, tiled=True)
+    key_piece, value_piece = jnp.split(
+        lax.all_gather(jnp.concatenate([key_send, value_send], axis=0), "blk", axis=1, tiled=True),
+        [key_send.shape[0]],
+        axis=0,
+    )
     count = key_piece.shape[1]
     key_h = key_piece.reshape(seqs, count, HEADS, depth)
     value_h = value_piece.reshape(seqs, count, HEADS, depth)

time: 999 us -> 1240 us (1.24)
  waiting for transfers between devices: 400 us -> 610 us
  matrix products: 326 us -> 351 us
  local copies, waits for them, and re-layouts: 58.5 us -> 70.9 us
    all_gather x0 -> x1, waiting for transfers between devices: none -> 209 us  [body(): lax.all_gather(jnp.concatenate([key_send, value_send], axis=0), 'blk', ax...]
    all_gather x1, waiting for transfers between devices: 21.1 us -> 92.7 us  [body(): key_piece = lax.all_gather(key_send, 'blk', axis=1, tiled=True)]
    all_gather x1, waiting for transfers between devices: 50.5 us -> 0.01 us  [body(): value_piece = lax.all_gather(value_send, 'blk', axis=1, tiled=True)]
    dot_general x1 -> x2, matrix products: 21.8 us -> 42.6 us  [body(): jnp.einsum('sqhe,skhe->shqk', query_b, key_h, preferred_element_type=jnp....]
    all_gather x1, waiting for transfers between devices: 35.5 us -> 16.6 us  [body(): lax.all_gather(query_b.reshape(seqs, span, width), 'blk', axis=1, tiled=T...]
  transfers between devices with their start and end apart: 10 -> 11, of which waited for: 8 -> 7; matrix products, arithmetic and copies ran while one was open for 36% -> 34% of each run, Pallas kernels for 0% -> 0%
where the time goes in v1:
time: 1240 us; the launch traced here: 1230 us
  waiting for transfers between devices  610 us (49%)
  matrix products  351 us (28%)
  blocking collectives  118 us (10%)
  local copies, waits for them, and re-layouts  70.9 us (6%)
  other arithmetic  66.4 us (5%)
  between operations  15.7 us (1%)
    all_gather x1, waiting for transfers between devices, body(): lax.all_gather(jnp.concatenate([key_send, value_send], axis=0), 'blk', ax...  209 us
    psum x1, waiting for transfers between devices, body(): lax.psum((grad_a_part, grad_a_ffp, grad_b_part, grad_b_ffp, gain_part, sh...  104 us
    all_gather x1, waiting for transfers between devices, body(): key_piece = lax.all_gather(key_send, 'blk', axis=1, tiled=True)  92.7 us
    all_gather x1, waiting for transfers between devices, body(): lax.all_gather(grad_att.reshape(seqs, span, width), 'blk', axis=1, tiled=...  92 us
    dot_general x12, matrix products, matrix_product(): return jnp.dot(left, right, preferred_element_type=jnp.float32)  91.7 us
    all_gather x1, waiting for transfers between devices, body(): lax.all_gather(shards[0], 'dp', axis=0, tiled=True)  74.9 us
    dot_general x12, matrix products, product_right_transposed(): lax.dot_general(left, right, (((1,), (1,)), ((), ())), preferred_element_...  74.3 us
    dot_general x2, matrix products, body(): jnp.einsum('sqhe,skhe->shqk', query_b, key_h, preferred_element_type=jnp....  42.6 us
  transfers between devices with their start and end apart: 11, of which 7 were waited for; matrix products, arithmetic and copies ran while one was open for 34% of the time, Pallas kernels for 0%

profile of v1, /device:TPU:0, one launch (start us, length us, event | category | flops | bytes accessed | tf_op | source)
XLA Modules:
  0.0 1233.2 jit_solution(7462082447765560982)
XLA Ops:
  12.9 11.8 all_gather.46
  27.6 74.9 %all-gather.11.cloned.1.call-done = bf16[1024,8192]{1,0:T(8,128)(2,1)} async-done(((bf16[128,8192]{1,0:T(8,128)(2,1)}), bf16[1024,8192]{1,0:T(8,128)(2,1)}) %all-gather.11.cloned.1.call-update) | async-done | bytes 16777232 | tf_op jit(solution)/shard_map/all_gather | solution.py:161
  112.7 20.2 %all-gather.13.cloned.1.call-done = bf16[128,8192]{1,0:T(8,128)(2,1)} async-done(((bf16[128,1024]{1,0:T(8,128)(2,1)}), bf16[128,8192]{1,0:T(8,128)(2,1)}) %all-gather.13.cloned.1.call-update) | async-done | bytes 2097168 | tf_op jit(solution)/shard_map/all_gather | solution.py:165
  197.4 12.8 %fusion.139 = f32[768,4096]{1,0:T(8,128)} fusion(bf16[768,1024]{1,0:T(8,128)(2,1)S(1)} %fusion.29, bf16[4096,1024]{1,0:T(8,128)(2,1)} %all-gather.17.cloned.1.call-done), kind=kOutput, calls=%fused_computation.236 | convolution fusion | flops 6442450944 | bytes 22544384 | tf_op jit(solution)/shard_map/dot_general | solution.py:24
  227.8 31.8 %multiply_convert_fusion.2 = (bf16[768,4096]{1,0:T(8,128)(2,1)}, f32[768,4096]{1,0:T(8,128)}, f32[768,4096]{1,0:T(8,128)}) fusion(bf16[768,128]{1,0:T(8,128)(2,1)S(1)} %convolution_convert_fusion.1, bf16[128,8192]{1,0:T(8,128)(2,1)S(1)} %copy-done.61, f32[768,4096]{1,0:T(8,128)S(1)} %fusion.20, f32[4096]{0:T(1024)S(1)} %slice_convert_fusion), kind=kOutput, calls=%fused_computation.16 | convolution fusion | flops 1019215872 | bytes 45301760 | tf_op jit(solution)/shard_map/dot_general | solution.py:20
  259.6 18.3 %add_convert_fusion = bf16[768,4096]{1,0:T(8,128)(2,1)} fusion(f32[768,4096]{1,0:T(8,128)} %get-tuple-element.99, f32[768,4096]{1,0:T(8,128)} %fusion.139, f32[768,4096]{1,0:T(8,128)} %get-tuple-element.138, bf16[768,128]{1,0:T(8,128)(2,1)S(1)} %fusion.70, bf16[4096,128]{1,0:T(8,128)(2,1)} %all-gather.19.cloned.1.call-done), kind=kOutput, calls=%fused_computation.15 | convolution fusion | flops 852492288 | bytes 45285376 | tf_op jit(solution)/shard_map/dot_general | solution.py:24
  302.3 12.5 %fusion.138 = f32[768,1024]{1,0:T(8,128)} fusion(bf16[768,4096]{1,0:T(8,128)(2,1)} %get-tuple-element.98, bf16[4096,1024]{1,0:T(8,128)(2,1)} %all-gather.17.cloned.1.call-done), kind=kOutput, calls=%fused_computation.235 | convolution fusion | flops 6442450944 | bytes 17825792 | tf_op jit(solution)/shard_map/dot_general | solution.py:20
  314.8 16.6 %all-gather.25.cloned.1.call-done = bf16[3,1024,1024]{1,2,0:T(8,128)(2,1)} async-done(((bf16[3,256,1024]{1,2,0:T(8,128)(2,1)}), bf16[3,1024,1024]{1,2,0:T(8,128)(2,1)}) %all-gather.25.cloned.1.call-update) | async-done | bytes 6291472 | tf_op jit(solution)/shard_map/all_gather | solution.py:262
  331.4 21.8 %fusion.136 = f32[3,16,1024,256]{3,2,1,0:T(8,128)} fusion(bf16[3,1024,16,64]{1,3,2,0:T(8,128)(2,1)} %bitcast.182, bf16[3,256,16,48]{1,3,2,0:T(8,128)(2,1)S(1)} %copy-done.17, bf16[3,256,16,8]{1,3,2,0:T(8,128)(2,1)S(1)} %copy-done.42, bf16[3,256,16,8]{1,3,2,0:T(8,128)(2,1)S(1)} %copy-done.44), kind=kOutput, calls=%fused_computation.233 | convolution fusion | flops 1615331328 | bytes 58195968 | tf_op jit(solution)/shard_map/sqhe,skhe->shqk/dot_general | solution.py:268
  353.2 92.7 %all-gather.21.cloned.1.call-done = bf16[3,1024,1024]{1,2,0:T(8,128)(2,1)} async-done(((bf16[3,256,1024]{1,2,0:T(8,128)(2,1)}), bf16[3,1024,1024]{1,2,0:T(8,128)(2,1)}) %all-gather.21.cloned.1.call-update) | async-done | bytes 6291472 | tf_op jit(solution)/shard_map/all_gather | solution.py:240
  445.9 23.7 %fusion.137 = f32[3,16,256,1024]{3,2,1,0:T(8,128)} fusion(bf16[3,1024,16,64]{1,3,2,0:T(8,128)(2,1)} %bitcast.192, bf16[3,256,16,48]{1,3,2,0:T(8,128)(2,1)S(1)} %copy-done.6, bf16[3,256,16,8]{1,3,2,0:T(8,128)(2,1)S(1)} %copy-done.31, bf16[3,256,16,8]{1,3,2,0:T(8,128)(2,1)S(1)} %copy-done.29), kind=kOutput, calls=%fused_computation.234 | convolution fusion | flops 1615331328 | bytes 58195968 | tf_op jit(solution)/shard_map/sqhe,skhe->shqk/dot_general | solution.py:246
  469.6 92.0 %all-gather.27.cloned.1.call-done = bf16[3,1024,1024]{2,1,0:T(8,128)(2,1)} async-done(((bf16[3,256,1024]{2,1,0:T(8,128)(2,1)}), bf16[3,1024,1024]{2,1,0:T(8,128)(2,1)}) %all-gather.27.cloned.1.call-update) | async-done | bytes 6291472 | tf_op jit(solution)/shard_map/all_gather | solution.py:263
  570.4 208.7 %all-gather.15.cloned.1.call-done = bf16[6,1024,1024]{1,2,0:T(8,128)(2,1)} async-done(((bf16[6,256,1024]{1,2,0:T(8,128)(2,1)}), bf16[6,1024,1024]{1,2,0:T(8,128)(2,1)}) %all-gather.15.cloned.1.call-update) | async-done | bytes 12582928 | tf_op jit(solution)/shard_map/all_gather | solution.py:194
  787.7 18.9 %fusion = (f32[3,16,256]{2,1,0:T(8,128)S(1)}, f32[3,16,256,1024]{3,2,1,0:T(8,128)}) fusion(pred[256,1024]{1,0:T(8,128)(4,1)S(1)} %copy-done.8, bf16[3,1024,16,64]{1,3,2,0:T(8,128)(2,1)S(1)} %bitcast.175, bf16[3,256,16,48]{1,3,2,0:T(8,128)(2,1)S(1)} %copy-done.6, bf16[3,256,16,8]{1,3,2,0:T(8,128)(2,1)S(1)} %copy-done.31, ...), kind=kOutput, calls=%fused_computation.5 | convolution fusion | flops 1653067776 | bytes 58507264 | tf_op jit(solution)/shard_map/sqhe,skhe->shqk/dot_general | solution.py:202
  806.6 23.3 %fusion.2 = f32[3,16,256]{2,1,0:T(8,128)S(1)} fusion(f32[3,16,256,1024]{3,2,1,0:T(8,128)} %get-tuple-element.137, f32[3,16,256]{2,1,0:T(8,128)S(1)} %broadcast_maximum_fusion, pred[256,1024]{1,0:T(8,128)(4,1)S(1)} %copy-done.8), kind=kLoop, calls=%fused_computation.7 | loop fusion | flops 62902272 | bytes 50692096 | tf_op jit(solution)/shard_map/reduce_sum | solution.py:209
  829.9 18.0 %all_gather.55 = bf16[3,16,1024]{2,1,0:T(8,128)(2,1)S(1)} all-gather(bf16[3,16,256]{2,1,0:T(8,128)(2,1)S(1)} %get-tuple-element.96), channel_id=1, replica_groups=mesh['dp'=8,'blk'=4] {'blk'}, dimensions={2}, use_global_device_ids=true | all-gather | bytes 122880 | tf_op jit(solution)/shard_map/all_gather | solution.py:257
  847.9 21.8 %multiply_reduce_fusion = (f32[3,256,16]{1,2,0:T(8,128)S(1)}, bf16[3,256,16,64]{1,3,2,0:T(8,128)(2,1)S(1)}) fusion(bf16[3,256,16,64]{1,3,2,0:T(8,128)(2,1)S(1)} %copy-done.46, f32[3,256,16]{1,2,0:T(8,128)S(1)} %bitcast.206, bf16[3,1024,16,64]{1,3,2,0:T(8,128)(2,1)} %bitcast.203, f32[3,16,256,1024]{3,2,1,0:T(8,128)} %get-tuple-element.137, ...), kind=kOutput, calls=%fused_computation.88 | convolution fusion | flops 1677447168 | bytes 60178432 | tf_op jit(solution)/shard_map/shqk,skhe->sqhe/dot_general | solution.py:210
  869.7 27.7 %all_gather.57 = bf16[3,16,1024]{2,1,0:T(8,128)(2,1)S(1)} all-gather(bf16[3,16,256]{2,1,0:T(8,128)(2,1)S(1)} %bitcast_convert_fusion), channel_id=1, replica_groups=mesh['dp'=8,'blk'=4] {'blk'}, dimensions={2}, use_global_device_ids=true | all-gather | bytes 122880 | tf_op jit(solution)/shard_map/all_gather | solution.py:260
  900.4 28.4 %multiply_bitcast_fusion = f32[3,256,16,64]{1,3,2,0:T(8,128)} fusion(bf16[3,1024,16,64]{1,3,2,0:T(8,128)(2,1)} %bitcast.183, f32[3,16,1024,256]{3,2,1,0:T(8,128)} %fusion.136, bf16[3,1024,16,64]{1,3,2,0:T(8,128)(2,1)} %bitcast.194, bf16[3,256,16,64]{1,3,2,0:T(8,128)(2,1)S(1)} %bitcast.178, f32[3,16,1024]{2,1,0:T(8,128)S(1)} %convert_element_type.206, ...), kind=kOutput, calls=%fused_computation.85 | convolution fusion | flops 3297509376 | bytes 68288512 | tf_op jit(solution)/shard_map/shqk,sqhe->skhe/dot_general | solution.py:279
  932.4 20.5 %fusion.65 = bf16[3,256,16,64]{1,3,2,0:T(8,128)(2,1)} fusion(bf16[3,1024,16,64]{1,3,2,0:T(8,128)(2,1)} %bitcast.195, f32[3,16,1024,256]{3,2,1,0:T(8,128)} %fusion.136, f32[3,16,1024]{2,1,0:T(8,128)S(1)} %convert_element_type.203, pred[1024,256]{1,0:T(8,128)(4,1)S(1)} %copy-done.65), kind=kOutput, calls=%fused_computation.99 | convolution fusion | flops 1661730816 | bytes 58654720 | tf_op jit(solution)/shard_map/shqk,sqhe->skhe/dot_general | solution.py:273
  952.9 29.6 %multiply_bitcast_fusion.1 = f32[3,256,16,64]{1,3,2,0:T(8,128)} fusion(bf16[3,1024,16,64]{1,3,2,0:T(8,128)(2,1)} %bitcast.193, f32[3,16,256,1024]{3,2,1,0:T(8,128)} %fusion.137, bf16[3,256,16,64]{1,3,2,0:T(8,128)(2,1)} %copy.79, bf16[3,1024,16,64]{1,3,2,0:T(8,128)(2,1)} %bitcast.222, f32[3,16,256]{2,1,0:T(8,128)S(1)} %bitcast.215, ...), kind=kOutput, calls=%fused_computation.87 | convolution fusion | flops 3297509376 | bytes 67993600 | tf_op jit(solution)/shard_map/shqk,skhe->sqhe/dot_general | solution.py:254
  1013.8 13.3 %fusion.129 = (f32[1024]{0:T(1024)S(1)}, f32[768]{0:T(1024)S(1)}, f32[768]{0:T(1024)S(1)}, f32[1024]{0:T(1024)S(1)}, f32[768,1024]{1,0:T(8,128)S(1)}) fusion(f32[1024]{0:T(1024)S(1)} %bitcast.212, f32[768]{0:T(1024)S(1)} %copy-done.75, bf16[3,256,1024]{2,1,0:T(8,128)(2,1)S(1)} %copy-done.1, f32[768,1024]{1,0:T(8,128)S(1)} %convolution_add_fusion, ...), kind=kOutput, calls=%fused_computation.227 | convolution fusion | flops 6451097600 | bytes 25715712 | tf_op jit(solution)/shard_map/dot_general | solution.py:24
  1030.2 41.3 %all-reduce.6 = (f32[2,1024]{1,0:T(2,128)}, f32[2,1024]{1,0:T(2,128)}) all-reduce(f32[2,1024]{1,0:T(2,128)S(1)} %pad_maximum_fusion.3, f32[2,1024]{1,0:T(2,128)S(1)} %pad_maximum_fusion.4), channel_id=1, replica_groups=mesh['dp'=8,'blk'=4] {'dp','blk'}, use_global_device_ids=true, to_apply=%region_12.13 | all-reduce | flops 4096 | bytes 32768 | tf_op jit(solution)/shard_map/psum | solution.py:301
  1079.7 103.6 %all-reduce.10.cloned.1.call-done = (f32[1024,384]{0,1:T(8,128)}, f32[4096,128]{1,0:T(8,128)}, f32[128,8192]{1,0:T(8,128)}, f32[128,1024]{1,0:T(8,128)}) async-done(((f32[1024,384]{0,1:T(8,128)}, f32[4096,128]{1,0:T(8,128)}, f32[128,8192]{1,0:T(8,128)}, f32[128,1024]{1,0:T(8,128)}), (f32[1024,384]{0,1:T(8,128)}, f32[4096,128]{1,0:T(8,128)}, f32[128,8192]{1,0:T(8,128)}, ...) | async-done | bytes 8388624 | tf_op jit(solution)/shard_map/psum | solution.py:301
  (338 shorter events, 233.4 us)
Async XLA Ops:
  7.2 95.3 %all-gather.11.cloned.1.call-start = ((), (), s32[]{:S(2)}) async-start(), calls=%async_computation | async-start | bytes 18874368 | tf_op jit(solution)/shard_map/all_gather | solution.py:161
  8.0 125.0 %all-gather.13.cloned.1.call-start = ((), (), s32[]{:S(2)}) async-start(), calls=%async_computation.1 | async-start | bytes 2359296 | tf_op jit(solution)/shard_map/all_gather | solution.py:165
  9.9 187.5 %all-gather.17.cloned.1.call-start = ((), (), s32[]{:S(2)}) async-start(), calls=%async_computation.3 | async-start | bytes 9437184 | tf_op jit(solution)/shard_map/all_gather | solution.py:162
  10.6 249.0 %all-gather.19.cloned.1.call-start = ((), (), s32[]{:S(2)}) async-start(), calls=%async_computation.4 | async-start | bytes 1179648 | tf_op jit(solution)/shard_map/all_gather | solution.py:164
  11.4 320.0 %all-gather.25.cloned.1.call-start = ((), (), s32[]{:S(2)}) async-start(), calls=%async_computation.7 | async-start | bytes 7864320 | tf_op jit(solution)/shard_map/all_gather | solution.py:262
  24.9 126.5 %copy-start.70 = (f32[256,8]{0,1:T(8,128)}, f32[256,8]{0,1:T(8,128)S(1)}, u32[]{:S(2)}) copy-start(f32[256,8]{0,1:T(8,128)S(1)} %get-tuple-element.134) | copy-start | bytes 24580
  24.9 126.4 %copy-start.72 = (f32[256,8]{0,1:T(8,128)}, f32[256,8]{0,1:T(8,128)S(1)}, u32[]{:S(2)}) copy-start(f32[256,8]{0,1:T(8,128)S(1)} %get-tuple-element.135) | copy-start | bytes 24580
  27.0 85.8 %copy-start.24 = (bf16[768,1024]{1,0:T(8,128)(2,1)}, bf16[768,1024]{1,0:T(8,128)(2,1)S(1)}, u32[]{:S(2)}) copy-start(bf16[768,1024]{1,0:T(8,128)(2,1)S(1)} %get-tuple-element.114) | copy-start | bytes 4718596
  27.6 105.4 %copy-start.52 = (bf16[768,128]{1,0:T(8,128)(2,1)}, bf16[768,128]{1,0:T(8,128)(2,1)S(1)}, u32[]{:S(2)}) copy-start(bf16[768,128]{1,0:T(8,128)(2,1)S(1)} %convolution_convert_fusion.3) | copy-start | bytes 589828
  154.5 291.4 %all-gather.21.cloned.1.call-start = ((), (), s32[]{:S(2)}) async-start(), calls=%async_computation.5 | async-start | bytes 7864320 | tf_op jit(solution)/shard_map/all_gather | solution.py:240
  158.9 402.7 %all-gather.27.cloned.1.call-start = ((), (), s32[]{:S(2)}) async-start(), calls=%async_computation.8 | async-start | bytes 7864320 | tf_op jit(solution)/shard_map/all_gather | solution.py:263
  159.6 140.8 %copy-start.9 = (bf16[768,1024]{1,0:T(8,128)(2,1)}, bf16[768,1024]{1,0:T(8,128)(2,1)S(1)}, u32[]{:S(2)}) copy-start(bf16[768,1024]{1,0:T(8,128)(2,1)S(1)} %fusion.29) | copy-start | bytes 4718596
  167.8 611.3 %all-gather.15.cloned.1.call-start = ((), (), s32[]{:S(2)}) async-start(), calls=%async_computation.2 | async-start | bytes 15728640 | tf_op jit(solution)/shard_map/all_gather | solution.py:194
  177.0 776.0 %all-gather.23.cloned.1.call-start = ((), (), s32[]{:S(2)}) async-start(), calls=%async_computation.6 | async-start | bytes 7864320 | tf_op jit(solution)/shard_map/all_gather | solution.py:241
  289.7 893.6 %all-reduce.10.cloned.1.call-start = ((), (), s32[]{:S(2)}) async-start(), calls=%async_computation.10 | async-start | bytes 16777216 | tf_op jit(solution)/shard_map/psum | solution.py:301
  331.4 114.5 %copy-start.6 = (bf16[3,256,16,48]{1,3,2,0:T(8,128)(2,1)S(1)}, bf16[3,256,16,48]{1,3,2,0:T(8,128)(2,1)}, u32[]{:S(2)}) copy-start(bf16[3,256,16,48]{1,3,2,0:T(8,128)(2,1)} %copy-done.5) | copy-start | bytes 3538948
  331.4 114.5 %copy-start.29 = (bf16[3,256,16,8]{1,3,2,0:T(8,128)(2,1)S(1)}, bf16[3,256,16,8]{1,3,2,0:T(8,128)(2,1)}, u32[]{:S(2)}) copy-start(bf16[3,256,16,8]{1,3,2,0:T(8,128)(2,1)} %copy-done.28) | copy-start | bytes 589828
  331.4 114.5 %copy-start.31 = (bf16[3,256,16,8]{1,3,2,0:T(8,128)(2,1)S(1)}, bf16[3,256,16,8]{1,3,2,0:T(8,128)(2,1)}, u32[]{:S(2)}) copy-start(bf16[3,256,16,8]{1,3,2,0:T(8,128)(2,1)} %copy-done.30) | copy-start | bytes 589828
  570.4 217.3 %copy-start.8 = (pred[256,1024]{1,0:T(8,128)(4,1)S(1)}, pred[256,1024]{1,0:T(8,128)(4,1)}, u32[]{:S(2)}) copy-start(pred[256,1024]{1,0:T(8,128)(4,1)} %iota_compare_fusion.1) | copy-start | bytes 786436
  1002.4 217.4 %all-gather.29.cloned.1.call-start = ((), (), s32[]{:S(2)}) async-start(), calls=%async_computation.9 | async-start | bytes 2359296 | tf_op jit(solution)/shard_map/all_gather | solution.py:324
  1079.7 106.2 %copy-start.48 = (bf16[128,1024]{1,0:T(8,128)(2,1)S(1)}, bf16[128,1024]{1,0:T(8,128)(2,1)}, u32[]{:S(2)}) copy-start(bf16[128,1024]{1,0:T(8,128)(2,1)} %copy-done.47) | copy-start | bytes 786436
  1079.7 106.2 %copy-start.60 = (bf16[768,128]{1,0:T(8,128)(2,1)S(1)}, bf16[768,128]{1,0:T(8,128)(2,1)}, u32[]{:S(2)}) copy-start(bf16[768,128]{1,0:T(8,128)(2,1)} %copy-done.59) | copy-start | bytes 589828
  1079.7 106.2 %copy-start.86 = (f32[1024]{0:T(1024)S(1)}, f32[1024]{0:T(1024)}, u32[]{:S(2)}) copy-start(f32[1024]{0:T(1024)} %convert_element_type.191) | copy-start | bytes 12292
  1079.7 106.2 %copy-start.87 = (f32[1024]{0:T(1024)S(1)}, f32[1024]{0:T(1024)}, u32[]{:S(2)}) copy-start(f32[1024]{0:T(1024)} %slice_convert_fusion.2) | copy-start | bytes 12292
  (84 other events, 704.2 us)
Sparse Core Ops, SparseCore 0:
  9.9 92.5 all-gather.10
  105.0 27.8 all-gather.12
  134.8 54.3 all-gather.16
  191.6 23.4 all-gather.18
  216.5 114.8 all-gather.24
  332.8 113.0 all-gather.20
  448.0 113.5 all-gather.26
  563.2 215.8 all-gather.14
  780.6 116.2 all-gather.22
  1002.6 180.6 all-reduce.9
  1186.0 28.6 all-gather.28
